TPU v7x, 32 devices: a whole 2x2x4 slice. The times are simulated.
32 devices in a mesh: acct: 8 (over z, y), rep: 4 (over x, core).
Axes of the slice: x: 2, y: 2, z: 4, core: 2. Of those that a mesh axis runs over, the one named last changes fastest.
Arguments:
- memory: bfloat16 [262144, 256], P(('acct', 'rep')), may hold values from -4 to 4
- features: bfloat16 [4096, 128], P(('acct', 'rep')), may hold values from -6 to 6
- buckets: int32 [4096], P(('acct', 'rep')), may hold values from 0 to 4095
- src_owner: int32 [4096, 1], P(('acct', 'rep')), may hold values from 0 to 31; in each aligned block of 128 rows (0 to 127, 128 to 255, ...) at most 8 rows name the same one
- src_slot: int32 [4096], P(('acct', 'rep')), may hold values from 0 to 8191
- dst_owner: int32 [4096, 1], P(('acct', 'rep')), may hold values from 0 to 31; in each aligned block of 128 rows (0 to 127, 128 to 255, ...) at most 8 rows name the same one
- dst_slot: int32 [4096], P(('acct', 'rep')), may hold values from 0 to 8191
- nb_owner: int32 [4096, 10, 1], P(('acct', 'rep')), may hold values from 0 to 31; in each aligned block of 1280 rows (0 to 1279, 1280 to 2559, ..., all dimensions but the last counted through in order) at most 80 rows name the same one
- nb_slot: int32 [4096, 10], P(('acct', 'rep')), may hold values from 0 to 8191
- w_msg: bfloat16 [512, 128], replicated, may hold values from -0.25 to 0.25
- w_in: bfloat16 [128, 768], replicated, may hold values from -0.5 to 0.5
- u_zr: bfloat16 [256, 512], replicated, may hold values from -0.375 to 0.375
- u_h: bfloat16 [256, 256], replicated, may hold values from -0.375 to 0.375
- w_query: bfloat16 [256, 256], replicated, may hold values from -0.375 to 0.375
- w_key: bfloat16 [256, 256], replicated, may hold values from -0.375 to 0.375
- w_value: bfloat16 [256, 256], replicated, may hold values from -0.375 to 0.375
- emb_grad: bfloat16 [4096, 256], P(('acct', 'rep')), may hold values from -6 to 6
Outputs:
- new_memory: bfloat16 [262144, 256], P(('acct', 'rep'))
- embedding: bfloat16 [4096, 256], P(('acct', 'rep'))
- grad_msg: float32 [512, 128], replicated
- grad_in: float32 [128, 768], replicated
- grad_zr: float32 [256, 512], replicated
- grad_h: float32 [256, 256], replicated
- grad_query: float32 [256, 256], replicated
- grad_key: float32 [256, 256], replicated
- grad_value: float32 [256, 256], replicated
Inputs may be any that keep to these rules, and one draw needn't show every extreme that they name: `src_owner`: in each aligned block of 128 events (one device's events) at most 8 events name one owner, a bound that some block reaches. `dst_owner`: in each aligned block of 128 events at most 8 events name one owner, a bound that some block reaches. `nb_owner`: in each aligned block of 128 events (1280 entries) at most 80 entries name one owner, a bound that some block reaches.
All inputs are finite; a program needn't handle non-finite values.
Results may differ from a plain program's by a relative error of at most 0.01.
Values may be sent and summed in bfloat16 or wider, within the bound.
No kernel may reach another device: no remote copies, remote signals or barrier semaphores. Data moves between devices by JAX's collectives and lax.ppermute only.
A program may use at most 192 MiB of HBM per device.

v0:
```python
import math
import jax
import jax.numpy as jnp
from jax import lax
from jax.sharding import PartitionSpec as P

HEADS = 2
cap_value = 10.0


def widen(tensor):
    return lax.optimization_barrier(tensor).astype(jnp.float32)


def time_code(buckets, code_width):
    column = jnp.arange(code_width, dtype=jnp.float32)
    frequency = jnp.exp(column * (-11.5 / code_width))
    return jnp.cos(buckets.astype(jnp.float32)[:, None] * frequency[None, :])


def message_forward(own_rows, features, buckets, w_msg):
    code_width = w_msg.shape[0] - own_rows.shape[1] - features.shape[1]
    encoded = time_code(buckets, code_width).astype(jnp.bfloat16)
    inputs = jnp.concatenate([own_rows, features, encoded], axis=1)
    pre_act = jnp.dot(inputs, w_msg, preferred_element_type=jnp.float32)
    message = jax.nn.silu(pre_act).astype(jnp.bfloat16)
    return (inputs, pre_act, message)


def message_backward(inputs, pre_act, d_message):
    sigmoid_pre = jax.nn.sigmoid(pre_act)
    d_pre = (d_message * sigmoid_pre * (1.0 + pre_act * (1.0 - sigmoid_pre))).astype(jnp.bfloat16)
    return jnp.dot(inputs.T, d_pre, preferred_element_type=jnp.float32)


def gru_forward(mean_rows, state_rows, touched, w_in, u_zr, u_h):
    row_width = state_rows.shape[1]
    from_input = jnp.dot(mean_rows, w_in, preferred_element_type=jnp.float32)
    from_state = jnp.dot(state_rows, u_zr, preferred_element_type=jnp.float32)
    update_gate = jax.nn.sigmoid(from_input[:, :row_width] + from_state[:, :row_width])
    reset_gate = jax.nn.sigmoid(
        from_input[:, row_width : 2 * row_width] + from_state[:, row_width:]
    )
    state_wide = state_rows.astype(jnp.float32)
    reset_state = (reset_gate * state_wide).astype(jnp.bfloat16)
    candidate = jnp.tanh(
        from_input[:, 2 * row_width :]
        + jnp.dot(reset_state, u_h, preferred_element_type=jnp.float32)
    )
    updated = (1.0 - update_gate) * state_wide + update_gate * candidate
    new_rows = jnp.where(touched[:, None], updated, state_wide).astype(jnp.bfloat16)
    return (new_rows, (update_gate, reset_gate, candidate, reset_state, state_wide))


def gru_backward(d_rows, touched, kept_values, mean_rows, state_rows, w_in, u_h):
    update_gate, reset_gate, candidate, reset_state, state_wide = kept_values
    row_width = state_rows.shape[1]
    d_updated = jnp.where(touched[:, None], d_rows, jnp.zeros_like(d_rows))
    d_update = d_updated * (candidate - state_wide)
    d_candidate = (d_updated * update_gate * (1.0 - candidate * candidate)).astype(jnp.bfloat16)
    grad_h = jnp.dot(reset_state.T, d_candidate, preferred_element_type=jnp.float32)
    d_reset_state = jnp.dot(d_candidate, u_h.T, preferred_element_type=jnp.float32)
    d_reset = d_reset_state * state_wide * reset_gate * (1.0 - reset_gate)
    d_update_in = d_update * update_gate * (1.0 - update_gate)
    d_gates = jnp.concatenate(
        [d_update_in.astype(jnp.bfloat16), d_reset.astype(jnp.bfloat16), d_candidate], axis=1
    )
    grad_in = jnp.dot(mean_rows.T, d_gates, preferred_element_type=jnp.float32)
    grad_zr = jnp.dot(state_rows.T, d_gates[:, : 2 * row_width], preferred_element_type=jnp.float32)
    d_mean = jnp.dot(d_gates, w_in.T, preferred_element_type=jnp.float32)
    return (d_mean, grad_in, grad_zr, grad_h)


def attend(q_rows, k_rows, w_query, w_key, w_value, upstream):
    batch_rows, row_width = q_rows.shape
    neighbours = k_rows.shape[1]
    head_size = row_width // HEADS
    scaling = 1.0 / math.sqrt(head_size)
    flat_keys = k_rows.reshape(batch_rows * neighbours, row_width)
    query_proj = jnp.dot(q_rows, w_query, preferred_element_type=jnp.float32).astype(jnp.bfloat16)
    key_proj = jnp.dot(flat_keys, w_key, preferred_element_type=jnp.float32).astype(jnp.bfloat16)
    value_proj = jnp.dot(flat_keys, w_value, preferred_element_type=jnp.float32).astype(
        jnp.bfloat16
    )
    q_heads = widen(query_proj).reshape(batch_rows, HEADS, head_size)
    k_heads = widen(key_proj).reshape(batch_rows, neighbours, HEADS, head_size)
    v_heads = widen(value_proj).reshape(batch_rows, neighbours, HEADS, head_size)
    raw_scores = jnp.einsum("bhd,bkhd->bhk", q_heads, k_heads) * scaling
    capped = jnp.tanh(raw_scores / cap_value)
    weights = jnp.exp(cap_value * capped)
    attention = weights / jnp.sum(weights, axis=2, keepdims=True)
    attention_b = widen(attention.astype(jnp.bfloat16))
    mixture = jnp.einsum("bhk,bkhd->bhd", attention_b, v_heads).reshape(batch_rows, row_width)
    embedded = (q_rows.astype(jnp.float32) + mixture).astype(jnp.bfloat16)
    up_heads = upstream.reshape(batch_rows, HEADS, head_size)
    d_probs = jnp.einsum("bhd,bkhd->bhk", up_heads, v_heads)
    d_scores = attention * (d_probs - jnp.sum(attention * d_probs, axis=2, keepdims=True))
    d_raw = d_scores * (1.0 - capped * capped) * scaling
    d_query = (
        jnp.einsum("bhk,bkhd->bhd", d_raw, k_heads)
        .reshape(batch_rows, row_width)
        .astype(jnp.bfloat16)
    )
    d_keys = (
        jnp.einsum("bhk,bhd->bkhd", d_raw, q_heads)
        .reshape(batch_rows * neighbours, row_width)
        .astype(jnp.bfloat16)
    )
    d_values = (
        jnp.einsum("bhk,bhd->bkhd", attention_b, up_heads)
        .reshape(batch_rows * neighbours, row_width)
        .astype(jnp.bfloat16)
    )
    grad_query = jnp.dot(q_rows.T, d_query, preferred_element_type=jnp.float32)
    grad_key = jnp.dot(flat_keys.T, d_keys, preferred_element_type=jnp.float32)
    grad_value = jnp.dot(flat_keys.T, d_values, preferred_element_type=jnp.float32)
    d_q_rows = upstream + jnp.dot(d_query, w_query.T, preferred_element_type=jnp.float32)
    d_k_rows = (
        jnp.dot(d_keys, w_key.T, preferred_element_type=jnp.float32)
        + jnp.dot(d_values, w_value.T, preferred_element_type=jnp.float32)
    ).reshape(batch_rows, neighbours, row_width)
    return (embedded, d_q_rows, d_k_rows, grad_query, grad_key, grad_value)


def slot_positions(owners, devices):
    matches = (owners[:, None] == jnp.arange(devices, dtype=jnp.int32)[None, :]).astype(jnp.int32)
    before = jnp.cumsum(matches, axis=0) - matches
    return jnp.sum(before * matches, axis=1)


def body(
    memory,
    features,
    buckets,
    src_owner,
    src_slot,
    dst_owner,
    dst_slot,
    nb_owner,
    nb_slot,
    w_msg,
    w_in,
    u_zr,
    u_h,
    w_query,
    w_key,
    w_value,
    emb_grad,
):
    devices = lax.axis_size(("acct", "rep"))
    events, row_width = emb_grad.shape
    acc_rows = memory.shape[0]
    neighbours = nb_slot.shape[1]
    feat_width = features.shape[1]
    cap_event = 2 * events // devices
    cap_neigh = 2 * events * neighbours // devices
    src_owners = src_owner[:, 0]
    dst_owners = dst_owner[:, 0]
    nb_owners = nb_owner.reshape(-1)
    src_place = src_owners * cap_event + slot_positions(src_owners, devices)
    dst_place = dst_owners * cap_event + slot_positions(dst_owners, devices)
    nb_place = nb_owners * cap_neigh + slot_positions(nb_owners, devices)
    unused = jnp.full((devices * cap_event,), -1, jnp.int32)
    side_slots = jnp.stack(
        [
            unused.at[src_place].set(src_slot).reshape(devices, cap_event),
            unused.at[dst_place].set(dst_slot).reshape(devices, cap_event),
        ],
        axis=1,
    )
    zero_ints = jnp.zeros((devices * cap_event,), jnp.int32)
    side_times = jnp.stack(
        [
            zero_ints.at[src_place].set(buckets).reshape(devices, cap_event),
            zero_ints.at[dst_place].set(buckets).reshape(devices, cap_event),
        ],
        axis=1,
    )
    nb_requests = (
        jnp.full((devices * cap_neigh,), -1, jnp.int32)
        .at[nb_place]
        .set(nb_slot.reshape(-1))
        .reshape(devices, cap_neigh)
    )
    got_slots, got_times, got_neigh = (
        lax.all_to_all(side_slots, ("acct", "rep"), split_axis=0, concat_axis=0, tiled=True),
        lax.all_to_all(side_times, ("acct", "rep"), split_axis=0, concat_axis=0, tiled=True),
        lax.all_to_all(nb_requests, ("acct", "rep"), split_axis=0, concat_axis=0, tiled=True),
    )
    zero_rows = jnp.zeros((devices * cap_event, feat_width), jnp.bfloat16)
    side_feats = jnp.stack(
        [
            zero_rows.at[src_place].set(features).reshape(devices, cap_event, feat_width),
            zero_rows.at[dst_place].set(features).reshape(devices, cap_event, feat_width),
        ],
        axis=1,
    )
    got_feats = lax.all_to_all(side_feats, ("acct", "rep"), split_axis=0, concat_axis=0, tiled=True)
    slot_list = got_slots.reshape(-1)
    present = (slot_list >= 0).astype(jnp.float32)
    safe_slots = jnp.maximum(slot_list, 0)
    inputs, pre_act, message = message_forward(
        memory[safe_slots], got_feats.reshape(-1, feat_width), got_times.reshape(-1), w_msg
    )
    totals = jax.ops.segment_sum(
        message.astype(jnp.float32) * present[:, None], safe_slots, acc_rows
    )
    counts = jax.ops.segment_sum(present, safe_slots, acc_rows)
    divisor = jnp.maximum(counts, 1.0)[:, None]
    mean_rows = (totals / divisor).astype(jnp.bfloat16)
    touched = counts > 0.5
    new_memory, kept_values = gru_forward(mean_rows, memory, touched, w_in, u_zr, u_h)
    dst_rows_asked = jnp.maximum(got_slots[:, 1, :], 0)
    nb_rows_asked = jnp.maximum(got_neigh, 0)
    dst_reply = new_memory[dst_rows_asked]
    nb_reply = new_memory[nb_rows_asked]
    back_dst, back_nb = (
        lax.all_to_all(dst_reply, ("acct", "rep"), split_axis=0, concat_axis=0, tiled=True),
        lax.all_to_all(nb_reply, ("acct", "rep"), split_axis=0, concat_axis=0, tiled=True),
    )
    q_rows = back_dst.reshape(-1, row_width)[dst_place]
    k_rows = back_nb.reshape(-1, row_width)[nb_place].reshape(events, neighbours, row_width)
    embedding, d_q_rows, d_k_rows, grad_query, grad_key, grad_value = attend(
        q_rows, k_rows, w_query, w_key, w_value, emb_grad.astype(jnp.float32)
    )
    dst_grads = jnp.zeros((devices * cap_event, row_width), jnp.float32).at[dst_place].set(d_q_rows)
    nb_grads = (
        jnp.zeros((devices * cap_neigh, row_width), jnp.float32)
        .at[nb_place]
        .set(d_k_rows.reshape(-1, row_width))
    )
    got_dst_grads, got_nb_grads = (
        lax.all_to_all(
            dst_grads.reshape(devices, cap_event, row_width),
            ("acct", "rep"),
            split_axis=0,
            concat_axis=0,
            tiled=True,
        ),
        lax.all_to_all(
            nb_grads.reshape(devices, cap_neigh, row_width),
            ("acct", "rep"),
            split_axis=0,
            concat_axis=0,
            tiled=True,
        ),
    )
    d_memory = jax.ops.segment_sum(
        got_dst_grads.reshape(-1, row_width), dst_rows_asked.reshape(-1), acc_rows
    )
    d_memory = d_memory + jax.ops.segment_sum(
        got_nb_grads.reshape(-1, row_width), nb_rows_asked.reshape(-1), acc_rows
    )
    d_mean, grad_in, grad_zr, grad_h = gru_backward(
        d_memory, touched, kept_values, mean_rows, memory, w_in, u_h
    )
    d_message = (d_mean / divisor)[safe_slots] * present[:, None]
    grad_msg = message_backward(inputs, pre_act, d_message)
    grad_msg, grad_in, grad_zr, grad_h, grad_query, grad_key, grad_value = lax.psum(
        (grad_msg, grad_in, grad_zr, grad_h, grad_query, grad_key, grad_value), ("acct", "rep")
    )
    return (
        new_memory,
        embedding,
        grad_msg,
        grad_in,
        grad_zr,
        grad_h,
        grad_query,
        grad_key,
        grad_value,
    )


def solution(mesh):
    return jax.shard_map(
        body,
        mesh=mesh,
        in_specs=(
            P(("acct", "rep"), None),
            P(("acct", "rep"), None),
            P(("acct", "rep")),
            P(("acct", "rep"), None),
            P(("acct", "rep")),
            P(("acct", "rep"), None),
            P(("acct", "rep")),
            P(("acct", "rep"), None, None),
            P(("acct", "rep"), None),
            P(),
            P(),
            P(),
            P(),
            P(),
            P(),
            P(),
            P(("acct", "rep"), None),
        ),
        out_specs=(
            P(("acct", "rep"), None),
            P(("acct", "rep"), None),
            P(),
            P(),
            P(),
            P(),
            P(),
            P(),
            P(),
        ),
        check_vma=False,
    )
```

profile of v0, /device:TPU:0, one launch (start us, length us, event | category | flops | bytes accessed | tf_op | source)
XLA Modules:
  0.0 554.3 jit_solution(9245944277085125631)
XLA Ops:
  15.1 7.3 %all-to-all-start = ((s32[32,2,8]{2,1,0:T(2,128)}), s32[32,2,8]{2,1,0:T(2,128)S(1)}, u32[]{:S(2)}, u32[]{:S(2)}) async-start(s32[32,2,8]{2,1,0:T(2,128)} %copy.87), calls=%async_computation | async-start | bytes 65536 | tf_op jit(solution)/shard_map/all_to_all | solution.py:186
  29.2 9.1 %reduce-window.6 = s32[32,10,128]{2,1,0:T(8,128)S(1)} reduce-window(s32[32,10,128]{2,1,0:T(8,128)S(1)} %fusion.57, s32[]{:T(128)} %constant.17.clone.1), window={size=1x1x128 pad=0_0x0_0x127_0}, to_apply=%region_12.13 | reduce-window | flops 5201920 | bytes 327684 | tf_op jit(solution)/shard_map/reduce-window
  39.6 10.3 %fusion.117 = f32[8192,512]{0,1:T(8,128)} fusion(bf16[8192,256]{1,0:T(8,128)(2,1)} %param.17, bf16[256,512]{1,0:T(8,128)(2,1)S(1)} %copy-done), kind=kOutput, calls=%fused_computation.187 | convolution fusion | flops 2147483648 | bytes 21233664 | tf_op jit(solution)/shard_map/dot_general | solution.py:39
  50.0 6.4 %copy.91 = bf16[8192,256]{0,1:T(8,128)(2,1)} copy(bf16[8192,256]{1,0:T(8,128)(2,1)} %param.17) | data formatting | bytes 8388608 | tf_op args[0]
  57.3 5.3 scatter_custom_fusion.8
  63.2 5.8 %all-to-all-start.2 = ((s32[32,2,8]{2,1,0:T(2,128)}), s32[32,2,8]{2,1,0:T(2,128)S(1)}, u32[]{:S(2)}, u32[]{:S(2)}) async-start(s32[32,2,8]{2,1,0:T(2,128)} %copy.90), calls=%async_computation.2 | async-start | bytes 65536 | tf_op jit(solution)/shard_map/all_to_all | solution.py:187
  69.4 3.3 scatter_custom_fusion.2
  73.5 2.8 all-to-all-done.2
  76.3 3.3 all-to-all-start.1
  79.8 4.3 gather_fusion
  85.0 2.8 all-to-all-done.1
  87.8 3.1 all-to-all-start.4
  91.3 5.4 scatter_custom_fusion.7
  96.7 11.9 %fusion.113 = f32[8192,768]{0,1:T(8,128)} fusion(bf16[128,768]{1,0:T(8,128)(2,1)S(1)} %copy-done.27, f32[8192,128]{1,0:T(8,128)} %scatter_custom_fusion.7, f32[8192]{0:T(1024)S(1)} %broadcast_maximum_fusion), kind=kOutput, calls=%fused_computation.186 | convolution fusion | flops 1612709888 | bytes 29589504 | tf_op jit(solution)/shard_map/dot_general | solution.py:38
  108.6 19.9 %fusion.6 = (bf16[8192,256]{0,1:T(8,128)(2,1)}, f32[8192,256]{0,1:T(8,128)}) fusion(bf16[8192,256]{0,1:T(8,128)(2,1)S(1)} %copy-done.4, pred[8192]{0:T(1024)(128)(4,1)S(1)} %broadcast_compare_fusion, f32[8192,512]{0,1:T(8,128)} %fusion.117, f32[8192,768]{0,1:T(8,128)} %fusion.113, bf16[256,256]{1,0:T(8,128)(2,1)S(1)} %copy-done.44), kind=kOutput, calls=%fused_computation.32 | convolution fusion | flops 1113587712 | bytes 63053824 | tf_op jit(solution)/shard_map/dot_general | solution.py:48
  128.5 6.4 %copy.104 = bf16[8192,256]{1,0:T(8,128)(2,1)} copy(bf16[8192,256]{0,1:T(8,128)(2,1)} %get-tuple-element.71) | data formatting | bytes 8388608
  134.9 4.4 gather_fusion.1
  139.2 5.8 %all-to-all-start.3 = ((bf16[32,8,256]{2,1,0:T(8,128)(2,1)}), bf16[32,8,256]{2,1,0:T(8,128)(2,1)S(1)}, u32[]{:S(2)}, u32[]{:S(2)}) async-start(bf16[32,8,256]{2,1,0:T(8,128)(2,1)} %bitcast.11), calls=%async_computation.3 | async-start | bytes 262144 | tf_op jit(solution)/shard_map/all_to_all | solution.py:218
  145.8 9.6 %gather_fusion.3 = bf16[2560,256]{1,0:T(8,128)(2,1)} fusion(bf16[8192,256]{1,0:T(8,128)(2,1)} %copy.104, s32[3072]{0:T(1024)S(1)} %pad_clamp_fusion), kind=kCustom, calls=%fused_computation.3 | custom fusion | bytes 2631680 | tf_op jit(solution)/shard_map/gather | solution.py:216
  155.4 16.5 %all-to-all-start.5 = ((bf16[32,80,256]{2,1,0:T(8,128)(2,1)}), bf16[32,80,256]{2,1,0:T(8,128)(2,1)S(1)}, u32[]{:S(2)}, u32[]{:S(2)}) async-start(bf16[32,80,256]{2,1,0:T(8,128)(2,1)} %bitcast.15), calls=%async_computation.5 | async-start | bytes 2621440 | tf_op jit(solution)/shard_map/all_to_all | solution.py:219
  173.2 30.5 %all-to-all-done.5 = bf16[32,80,256]{2,1,0:T(8,128)(2,1)S(1)} async-done(((bf16[32,80,256]{2,1,0:T(8,128)(2,1)}), bf16[32,80,256]{2,1,0:T(8,128)(2,1)S(1)}, u32[]{:S(2)}, u32[]{:S(2)}) %all-to-all-start.5) | async-done | bytes 1310752 | tf_op jit(solution)/shard_map/all_to_all | solution.py:219
  203.7 4.1 gather_fusion.4
  213.4 1.7 scatter_custom_fusion.9
  215.1 3.6 all-to-all-start.6
  219.9 1.8 multiply_convert_fusion.1
  221.7 1.8 multiply_convert_fusion.2
  226.0 9.7 %scatter_custom_fusion.10 = f32[2560,256]{1,0:T(8,128)} fusion(s32[1280]{0:T(1024)} %copy-done.37, f32[1280,256]{1,0:T(8,128)S(1)} %convolution_add_fusion.1, f32[]{:T(128)} %constant.14.clone.1), kind=kCustom, calls=%fused_computation.66 | custom fusion | bytes 2621952 | tf_op jit(solution)/shard_map/scatter | solution.py:230
  235.7 5.8 %all-to-all-start.7 = ((f32[32,80,256]{2,1,0:T(8,128)}), f32[32,80,256]{2,1,0:T(8,128)S(1)}, u32[]{:S(2)}, u32[]{:S(2)}) async-start(f32[32,80,256]{2,1,0:T(8,128)} %bitcast.29), calls=%async_computation.7 | async-start | bytes 5242880 | tf_op jit(solution)/shard_map/all_to_all | solution.py:240
  244.4 1.8 fusion.69
  246.1 2.2 fusion.44
  248.3 2.2 fusion.47
  250.5 51.2 %all-to-all-done.7 = f32[32,80,256]{2,1,0:T(8,128)S(1)} async-done(((f32[32,80,256]{2,1,0:T(8,128)}), f32[32,80,256]{2,1,0:T(8,128)S(1)}, u32[]{:S(2)}, u32[]{:S(2)}) %all-to-all-start.7) | async-done | bytes 2621472 | tf_op jit(solution)/shard_map/all_to_all | solution.py:240
  301.7 23.0 %scatter_custom_fusion.11 = f32[8192,256]{1,0:T(8,128)} fusion(s32[2816]{0:T(1024)} %add_reduce_fusion, f32[]{:T(128)} %constant.14.clone.1, f32[2560,256]{1,0:T(8,128)S(1)} %bitcast.149, f32[]{:T(128)} %constant.74, f32[256,256]{1,0:T(8,128)S(1)} %bitcast.155), kind=kCustom, calls=%fused_computation.53 | custom fusion | flops 1441792 | bytes 11273216 | tf_op jit(solution)/shard_map/add | solution.py:251
  324.8 8.9 %copy.103 = f32[8192,256]{0,1:T(8,128)} copy(f32[8192,256]{1,0:T(8,128)} %scatter_custom_fusion.11) | data formatting | bytes 16777216 | tf_op jit(solution)/shard_map/add | solution.py:251
  333.7 17.8 %fusion.10 = (bf16[8192,256]{0,1:T(8,128)(2,1)}, bf16[8192,256]{0,1:T(8,128)(2,1)}) fusion(f32[8192,256]{0,1:T(8,128)} %get-tuple-element.72, bf16[8192,256]{0,1:T(8,128)(2,1)} %copy.91, f32[8192,256]{0,1:T(8,128)} %copy.103, pred[8192]{0:T(1024)(128)(4,1)S(1)} %copy-done.36, f32[8192,512]{0,1:T(8,128)} %fusion.117, f32[8192,768]{0,1:T(8,128)} %fusion.113), kind=kLoop, calls=%fused_computation.36 | loop fusion | flops 35651584 | bytes 46145536 | tf_op jit(solution)/shard_map/convert_element_type | solution.py:66
  351.5 10.3 %fusion.110 = f32[256,256]{1,0:T(8,128)} fusion(bf16[8192,256]{0,1:T(8,128)(2,1)} %get-tuple-element.64, bf16[8192,256]{0,1:T(8,128)(2,1)S(1)} %copy-done.5, f32[8192,512]{0,1:T(8,128)} %fusion.117, f32[8192,768]{0,1:T(8,128)} %fusion.113), kind=kOutput, calls=%fused_computation.185 | convolution fusion | flops 1088421888 | bytes 25427968 | tf_op jit(solution)/shard_map/dot_general | solution.py:61
  361.9 9.2 %fusion.3 = bf16[8192,256]{0,1:T(8,128)(2,1)} fusion(bf16[8192,256]{0,1:T(8,128)(2,1)S(1)} %copy-done.5, bf16[256,256]{1,0:T(8,128)(2,1)S(1)} %copy-done.45, bf16[8192,256]{0,1:T(8,128)(2,1)S(1)} %copy-done.7, f32[8192,512]{0,1:T(8,128)} %fusion.117, f32[8192,768]{0,1:T(8,128)} %fusion.113), kind=kOutput, calls=%fused_computation.28 | convolution fusion | flops 1094713344 | bytes 29491200 | tf_op jit(solution)/shard_map/dot_general | solution.py:62
  371.3 9.0 %fusion.23 = f32[128,768]{1,0:T(8,128)} fusion(bf16[8192,256]{0,1:T(8,128)(2,1)S(1)} %copy-done.7, bf16[8192,256]{0,1:T(8,128)(2,1)} %fusion.3, bf16[8192,256]{0,1:T(8,128)(2,1)S(1)} %copy-done.6, f32[8192,128]{1,0:T(8,128)S(1)} %copy-done.3, f32[8192]{0:T(1024)S(1)} %copy-done.26), kind=kOutput, calls=%fused_computation.52 | convolution fusion | flops 1650458624 | bytes 17203200 | tf_op jit(solution)/shard_map/dot_general | solution.py:68
  380.3 6.7 %convolution_divide_fusion = f32[8192,128]{1,0:T(8,128)} fusion(bf16[128,768]{1,0:T(8,128)(2,1)S(1)} %copy-done.28, bf16[8192,256]{0,1:T(8,128)(2,1)S(1)} %copy-done.8, bf16[8192,256]{0,1:T(8,128)(2,1)S(1)} %copy-done.46, bf16[8192,256]{0,1:T(8,128)(2,1)S(1)} %copy-done.6, f32[8192]{0:T(1024)S(1)} %copy-done.26), kind=kOutput, calls=%fused_computation.29 | convolution fusion | flops 1649410048 | bytes 17006592 | tf_op jit(solution)/shard_map/dot_general | solution.py:70
  387.0 5.4 fusion.33
  392.5 3.2 gather_fusion.5
  398.2 136.7 %all-reduce.3.cloned.1.call-done = (f32[512,128]{1,0:T(8,128)}, f32[128,768]{1,0:T(8,128)}, f32[256,512]{0,1:T(8,128)}, f32[256,256]{1,0:T(8,128)}, f32[256,256]...) async-done(((f32[512,128]{1,0:T(8,128)}, f32[128,768]{1,0:T(8,128)}, f32[256,512]{0,1:T(8,128)}, f32[256,256]{1,0:T(8,128)}, f32[256,256]{1,0:T(8,128)}, ...) | async-done | bytes 2228240 | tf_op jit(solution)/shard_map/psum | solution.py:259
  534.9 2.0 copy.105
  536.9 1.7 copy.164
  538.6 1.8 copy.165
  540.3 1.7 copy.166
  542.0 1.7 copy.167
  543.7 1.7 copy.168
  (195 shorter events, 38.1 us)
Async XLA Ops:
  7.2 32.5 %copy-start = (bf16[256,512]{1,0:T(8,128)(2,1)S(1)}, bf16[256,512]{1,0:T(8,128)(2,1)}, u32[]{:S(2)}) copy-start(bf16[256,512]{1,0:T(8,128)(2,1)} %param.28) | copy-start | bytes 786436
  15.1 48.1 %all-to-all-start = ((s32[32,2,8]{2,1,0:T(2,128)}), s32[32,2,8]{2,1,0:T(2,128)S(1)}, u32[]{:S(2)}, u32[]{:S(2)}) async-start(s32[32,2,8]{2,1,0:T(2,128)} %copy.87), calls=%async_computation | async-start | bytes 65536 | tf_op jit(solution)/shard_map/all_to_all | solution.py:186
  39.6 132.4 %copy-start.37 = (s32[1280]{0:T(1024)}, s32[1280]{0:T(1024)S(1)}, u32[]{:S(2)}) copy-start(s32[1280]{0:T(1024)S(1)} %fusion.91) | copy-start | bytes 15364
  49.9 41.1 %copy-start.43 = (bf16[512,128]{1,0:T(8,128)(2,1)S(1)}, bf16[512,128]{1,0:T(8,128)(2,1)}, u32[]{:S(2)}) copy-start(bf16[512,128]{1,0:T(8,128)(2,1)} %param.26) | copy-start | bytes 393220
  49.9 46.8 %copy-start.27 = (bf16[128,768]{1,0:T(8,128)(2,1)S(1)}, bf16[128,768]{1,0:T(8,128)(2,1)}, u32[]{:S(2)}) copy-start(bf16[128,768]{1,0:T(8,128)(2,1)} %param.27) | copy-start | bytes 589828
  63.2 13.1 %all-to-all-start.2 = ((s32[32,2,8]{2,1,0:T(2,128)}), s32[32,2,8]{2,1,0:T(2,128)S(1)}, u32[]{:S(2)}, u32[]{:S(2)}) async-start(s32[32,2,8]{2,1,0:T(2,128)} %copy.90), calls=%async_computation.2 | async-start | bytes 65536 | tf_op jit(solution)/shard_map/all_to_all | solution.py:187
  69.2 39.3 %copy-start.40 = (f32[512]{0:T(512)}, f32[512]{0:T(512)S(1)}, u32[]{:S(2)}) copy-start(f32[512]{0:T(512)S(1)} %reshape.286) | copy-start | bytes 6148
  72.7 35.8 %copy-start.35 = (pred[8192]{0:T(1024)(128)(4,1)}, pred[8192]{0:T(1024)(128)(4,1)S(1)}, u32[]{:S(2)}) copy-start(pred[8192]{0:T(1024)(128)(4,1)S(1)} %broadcast_compare_fusion) | copy-start | bytes 24580
  72.7 35.8 %copy-start.25 = (f32[8192]{0:T(1024)}, f32[8192]{0:T(1024)S(1)}, u32[]{:S(2)}) copy-start(f32[8192]{0:T(1024)S(1)} %broadcast_maximum_fusion) | copy-start | bytes 98308
  73.4 14.4 %copy-start.38 = (s32[1024]{0:T(1024)}, s32[1024]{0:T(1024)S(1)}, u32[]{:S(2)}) copy-start(s32[1024]{0:T(1024)S(1)} %pad_clamp_fusion.4) | copy-start | bytes 12292
  76.3 11.5 %all-to-all-start.1 = ((bf16[32,2,8,128]{3,2,1,0:T(8,128)(2,1)}), bf16[32,2,8,128]{3,2,1,0:T(8,128)(2,1)S(1)}, u32[]{:S(2)}, u32[]{:S(2)}) async-start(bf16[32,2,8,128]{3,2,1,0:T(8,128)(2,1)} %pad_maximum_fusion.6), calls=%async_computation.1 | async-start | bytes 262144 | tf_op jit(solution)/shard_map/all_to_all | solution.py:198
  84.1 24.5 %copy-start.23 = (bf16[512,256]{1,0:T(8,128)(2,1)}, bf16[512,256]{1,0:T(8,128)(2,1)S(1)}, u32[]{:S(2)}) copy-start(bf16[512,256]{1,0:T(8,128)(2,1)S(1)} %gather_fusion) | copy-start | bytes 786436
  85.0 23.6 %copy-start.31 = (bf16[512,128]{1,0:T(8,128)(2,1)}, bf16[512,128]{1,0:T(8,128)(2,1)S(1)}, u32[]{:S(2)}) copy-start(bf16[512,128]{1,0:T(8,128)(2,1)S(1)} %cosine_convert_fusion) | copy-start | bytes 393220
  87.8 20.8 %copy-start.29 = (bf16[32,2,8,128]{3,2,1,0:T(8,128)(2,1)}, bf16[32,2,8,128]{3,2,1,0:T(8,128)(2,1)S(1)}, u32[]{:S(2)}) copy-start(bf16[32,2,8,128]{3,2,1,0:T(8,128)(2,1)S(1)} %all-to-all-done.1) | copy-start | bytes 393220
  87.8 51.4 %all-to-all-start.4 = ((s32[32,1,80]{2,1,0:T(1,128)}), s32[32,1,80]{2,1,0:T(1,128)S(1)}, u32[]{:S(2)}, u32[]{:S(2)}) async-start(s32[32,1,80]{2,1,0:T(1,128)} %all_to_all.31), calls=%async_computation.4 | async-start | bytes 32768 | tf_op jit(solution)/shard_map/all_to_all | solution.py:188
  91.3 17.3 %copy-start.21 = (f32[512,128]{1,0:T(8,128)}, f32[512,128]{1,0:T(8,128)S(1)}, u32[]{:S(2)}) copy-start(f32[512,128]{1,0:T(8,128)S(1)} %fusion.59) | copy-start | bytes 786436
  96.7 11.9 %copy-start.4 = (bf16[8192,256]{0,1:T(8,128)(2,1)S(1)}, bf16[8192,256]{0,1:T(8,128)(2,1)}, u32[]{:S(2)}) copy-start(bf16[8192,256]{0,1:T(8,128)(2,1)} %copy.91) | copy-start | bytes 12582916
  96.7 11.9 %copy-start.44 = (bf16[256,256]{1,0:T(8,128)(2,1)S(1)}, bf16[256,256]{1,0:T(8,128)(2,1)}, u32[]{:S(2)}) copy-start(bf16[256,256]{1,0:T(8,128)(2,1)} %param.29) | copy-start | bytes 393220
  134.9 37.0 %copy-start.16 = (bf16[128,256]{1,0:T(8,128)(2,1)S(1)}, bf16[128,256]{1,0:T(8,128)(2,1)}, u32[]{:S(2)}) copy-start(bf16[128,256]{1,0:T(8,128)(2,1)} %param.33) | copy-start | bytes 196612
  134.9 38.0 %copy-start.18 = (bf16[256,256]{1,0:T(8,128)(2,1)S(1)}, bf16[256,256]{1,0:T(8,128)(2,1)}, u32[]{:S(2)}) copy-start(bf16[256,256]{1,0:T(8,128)(2,1)} %param.30) | copy-start | bytes 393220
  139.2 16.1 %all-to-all-start.3 = ((bf16[32,8,256]{2,1,0:T(8,128)(2,1)}), bf16[32,8,256]{2,1,0:T(8,128)(2,1)S(1)}, u32[]{:S(2)}, u32[]{:S(2)}) async-start(bf16[32,8,256]{2,1,0:T(8,128)(2,1)} %bitcast.11), calls=%async_computation.3 | async-start | bytes 262144 | tf_op jit(solution)/shard_map/all_to_all | solution.py:218
  145.8 61.9 %copy-start.20 = (bf16[256,256]{1,0:T(8,128)(2,1)S(1)}, bf16[256,256]{1,0:T(8,128)(2,1)}, u32[]{:S(2)}) copy-start(bf16[256,256]{1,0:T(8,128)(2,1)} %param.32) | copy-start | bytes 393220
  155.4 53.6 %copy-start.19 = (bf16[256,256]{1,0:T(8,128)(2,1)S(1)}, bf16[256,256]{1,0:T(8,128)(2,1)}, u32[]{:S(2)}) copy-start(bf16[256,256]{1,0:T(8,128)(2,1)} %param.31) | copy-start | bytes 393220
  155.4 48.3 %all-to-all-start.5 = ((bf16[32,80,256]{2,1,0:T(8,128)(2,1)}), bf16[32,80,256]{2,1,0:T(8,128)(2,1)S(1)}, u32[]{:S(2)}, u32[]{:S(2)}) async-start(bf16[32,80,256]{2,1,0:T(8,128)(2,1)} %bitcast.15), calls=%async_computation.5 | async-start | bytes 2621440 | tf_op jit(solution)/shard_map/all_to_all | solution.py:219
  172.9 38.6 %copy-start.11 = (bf16[128,256]{1,0:T(8,128)(2,1)}, bf16[128,256]{1,0:T(8,128)(2,1)S(1)}, u32[]{:S(2)}) copy-start(bf16[128,256]{1,0:T(8,128)(2,1)S(1)} %gather_fusion.2) | copy-start | bytes 196612
  215.1 20.6 %all-to-all-start.6 = ((f32[32,8,256]{2,1,0:T(8,128)}), f32[32,8,256]{2,1,0:T(8,128)S(1)}, u32[]{:S(2)}, u32[]{:S(2)}) async-start(f32[32,8,256]{2,1,0:T(8,128)} %bitcast.25), calls=%async_computation.6 | async-start | bytes 524288 | tf_op jit(solution)/shard_map/all_to_all | solution.py:233
  219.9 21.7 %copy-start.33 = (s32[32,1,8]{2,1,0:T(1,128)S(1)}, s32[32,1,8]{2,1,0:T(1,128)}, u32[]{:S(2)}) copy-start(s32[32,1,8]{2,1,0:T(1,128)} %get-tuple-element.65) | copy-start | bytes 3076
  235.7 66.0 %all-to-all-start.7 = ((f32[32,80,256]{2,1,0:T(8,128)}), f32[32,80,256]{2,1,0:T(8,128)S(1)}, u32[]{:S(2)}, u32[]{:S(2)}) async-start(f32[32,80,256]{2,1,0:T(8,128)} %bitcast.29), calls=%async_computation.7 | async-start | bytes 5242880 | tf_op jit(solution)/shard_map/all_to_all | solution.py:240
  241.5 293.3 %all-reduce.3.cloned.1.call-start = ((), (), s32[]{:S(2)}) async-start(), calls=%async_computation.8 | async-start | bytes 4456448 | tf_op jit(solution)/shard_map/psum | solution.py:259
  324.7 8.9 %copy-start.36 = (pred[8192]{0:T(1024)(128)(4,1)S(1)}, pred[8192]{0:T(1024)(128)(4,1)}, u32[]{:S(2)}) copy-start(pred[8192]{0:T(1024)(128)(4,1)} %copy-done.35) | copy-start | bytes 24580
  333.7 17.8 %copy-start.5 = (bf16[8192,256]{0,1:T(8,128)(2,1)S(1)}, bf16[8192,256]{0,1:T(8,128)(2,1)}, u32[]{:S(2)}) copy-start(bf16[8192,256]{0,1:T(8,128)(2,1)} %copy.91) | copy-start | bytes 12582916
  351.5 10.3 %copy-start.7 = (bf16[8192,256]{0,1:T(8,128)(2,1)S(1)}, bf16[8192,256]{0,1:T(8,128)(2,1)}, u32[]{:S(2)}) copy-start(bf16[8192,256]{0,1:T(8,128)(2,1)} %get-tuple-element.64) | copy-start | bytes 12582916
  351.5 10.3 %copy-start.45 = (bf16[256,256]{1,0:T(8,128)(2,1)S(1)}, bf16[256,256]{1,0:T(8,128)(2,1)}, u32[]{:S(2)}) copy-start(bf16[256,256]{1,0:T(8,128)(2,1)} %param.29) | copy-start | bytes 393220
  361.8 9.2 %copy-start.3 = (f32[8192,128]{1,0:T(8,128)S(1)}, f32[8192,128]{1,0:T(8,128)}, u32[]{:S(2)}) copy-start(f32[8192,128]{1,0:T(8,128)} %scatter_custom_fusion.7) | copy-start | bytes 12582916
  361.8 9.4 %copy-start.6 = (bf16[8192,256]{0,1:T(8,128)(2,1)S(1)}, bf16[8192,256]{0,1:T(8,128)(2,1)}, u32[]{:S(2)}) copy-start(bf16[8192,256]{0,1:T(8,128)(2,1)} %get-tuple-element.63) | copy-start | bytes 12582916
  361.8 9.4 %copy-start.26 = (f32[8192]{0:T(1024)S(1)}, f32[8192]{0:T(1024)}, u32[]{:S(2)}) copy-start(f32[8192]{0:T(1024)} %copy-done.25) | copy-start | bytes 98308
  371.3 9.0 %copy-start.8 = (bf16[8192,256]{0,1:T(8,128)(2,1)S(1)}, bf16[8192,256]{0,1:T(8,128)(2,1)}, u32[]{:S(2)}) copy-start(bf16[8192,256]{0,1:T(8,128)(2,1)} %get-tuple-element.64) | copy-start | bytes 12582916
  371.3 9.0 %copy-start.28 = (bf16[128,768]{1,0:T(8,128)(2,1)S(1)}, bf16[128,768]{1,0:T(8,128)(2,1)}, u32[]{:S(2)}) copy-start(bf16[128,768]{1,0:T(8,128)(2,1)} %param.27) | copy-start | bytes 589828
  371.3 9.0 %copy-start.46 = (bf16[8192,256]{0,1:T(8,128)(2,1)S(1)}, bf16[8192,256]{0,1:T(8,128)(2,1)}, u32[]{:S(2)}) copy-start(bf16[8192,256]{0,1:T(8,128)(2,1)} %fusion.3) | copy-start | bytes 12582916
  380.3 6.7 %copy-start.2 = (bf16[8192,256]{1,0:T(8,128)(2,1)S(1)}, bf16[8192,256]{1,0:T(8,128)(2,1)}, u32[]{:S(2)}) copy-start(bf16[8192,256]{1,0:T(8,128)(2,1)} %param.17) | copy-start | bytes 12582916
  387.0 8.8 %copy-start.22 = (f32[512,128]{1,0:T(8,128)S(1)}, f32[512,128]{1,0:T(8,128)}, u32[]{:S(2)}) copy-start(f32[512,128]{1,0:T(8,128)} %copy-done.21) | copy-start | bytes 786436
  387.0 8.8 %copy-start.24 = (bf16[512,256]{1,0:T(8,128)(2,1)S(1)}, bf16[512,256]{1,0:T(8,128)(2,1)}, u32[]{:S(2)}) copy-start(bf16[512,256]{1,0:T(8,128)(2,1)} %copy-done.23) | copy-start | bytes 786436
  387.0 8.8 %copy-start.30 = (bf16[32,2,8,128]{3,2,1,0:T(8,128)(2,1)S(1)}, bf16[32,2,8,128]{3,2,1,0:T(8,128)(2,1)}, u32[]{:S(2)}) copy-start(bf16[32,2,8,128]{3,2,1,0:T(8,128)(2,1)} %copy-done.29) | copy-start | bytes 393220
  387.0 8.8 %copy-start.32 = (bf16[512,128]{1,0:T(8,128)(2,1)S(1)}, bf16[512,128]{1,0:T(8,128)(2,1)}, u32[]{:S(2)}) copy-start(bf16[512,128]{1,0:T(8,128)(2,1)} %copy-done.31) | copy-start | bytes 393220
  387.0 8.8 %copy-start.41 = (f32[512]{0:T(512)S(1)}, f32[512]{0:T(512)}, u32[]{:S(2)}) copy-start(f32[512]{0:T(512)} %copy-done.40) | copy-start | bytes 6148
  387.0 9.9 %copy-start.34 = (bf16[128,2,10]{0,1,2:T(2,128)(2,1)S(1)}, bf16[128,2,10]{0,1,2:T(2,128)(2,1)}, u32[]{:S(2)}) copy-start(bf16[128,2,10]{0,1,2:T(2,128)(2,1)} %get-tuple-element.70) | copy-start | bytes 15364
  387.0 10.1 %copy-start.14 = (bf16[128,10,2,128]{3,2,1,0:T(2,128)(2,1)S(1)}, bf16[128,10,2,128]{3,2,1,0:T(2,128)(2,1)}, u32[]{:S(2)}) copy-start(bf16[128,10,2,128]{3,2,1,0:T(2,128)(2,1)} %copy-done.13) | copy-start | bytes 1966084
  387.0 160.0 %copy-start.1 = (bf16[256,512]{1,0:T(8,128)(2,1)S(1)}, bf16[256,512]{1,0:T(8,128)(2,1)}, u32[]{:S(2)}) copy-start(bf16[256,512]{1,0:T(8,128)(2,1)} %param.28) | copy-start | bytes 786436
  (8 other events, 26.9 us)
Sparse Core Ops, SparseCore 0:
  397.1 137.7 all-reduce.2
where the time goes:
time: 563 us; the launch traced here: 554 us
  waiting for transfers between devices  224 us (40%)
  matrix products  96 us (17%)
  local copies, waits for them, and re-layouts  93.5 us (17%)
  other arithmetic  73.9 us (13%)
  starting transfers between devices  51.4 us (9%)
  between operations  15.4 us (3%)
    psum x1, waiting for transfers between devices, body(): lax.psum((grad_msg, grad_in, grad_zr, grad_h, grad_query, grad_key, grad_...  137 us
    all_to_all x1, waiting for transfers between devices, body(): lax.all_to_all(nb_grads.reshape(devices, cap_neigh, row_width), ('acct',...  51.2 us
    all_to_all x1, waiting for transfers between devices, body(): lax.all_to_all(nb_reply, ('acct', 'rep'), split_axis=0, concat_axis=0, ti...  30.5 us
    unnamed x105, local copies, waits for them, and re-layouts  27 us
    add x1, other arithmetic, body(): d_memory + jax.ops.segment_sum(got_nb_grads.reshape(-1, row_width), nb_ro...  23 us
    dot_general x1, matrix products, gru_forward(): jnp.dot(reset_state, u_h, preferred_element_type=jnp.float32)  19.9 us
    convert_element_type x1, other arithmetic, gru_backward(): d_update_in.astype(jnp.bfloat16)  17.8 us
    all_to_all x1, starting transfers between devices, body(): lax.all_to_all(nb_reply, ('acct', 'rep'), split_axis=0, concat_axis=0, ti...  16.5 us
  transfers between devices with their start and end apart: 9, of which 5 were waited for; matrix products, arithmetic and copies ran while one was open for 24% of the time, Pallas kernels for 0%

commit v1 on v0

--- a/solution.py
+++ b/solution.py
@@ -257,7 +257,8 @@
     d_message = (d_mean / divisor)[safe_slots] * present[:, None]
     grad_msg = message_backward(inputs, pre_act, d_message)
     grad_msg, grad_in, grad_zr, grad_h, grad_query, grad_key, grad_value = lax.psum(
-        (grad_msg, grad_in, grad_zr, grad_h, grad_query, grad_key, grad_value), ("acct", "rep")
+        lax.psum((grad_msg, grad_in, grad_zr, grad_h, grad_query, grad_key, grad_value), "rep"),
+        "acct",
     )
     return (
         new_memory,

time: 563 us -> 594 us (1.055)
  waiting for transfers between devices: 224 us -> 254 us
    psum x0 -> x1, waiting for transfers between devices: none -> 112 us  [body(): lax.psum(lax.psum((grad_msg, grad_in, grad_zr, grad_h, grad_query, grad_k...]
    psum x1, waiting for transfers between devices: 137 us -> 54.8 us  [body(): lax.psum((grad_msg, grad_in, grad_zr, grad_h, grad_query, grad_key, grad_...]
  transfers between devices with their start and end apart: 9 -> 10, of which waited for: 5 -> 6; matrix products, arithmetic and copies ran while one was open for 24% -> 23% of each run, Pallas kernels for 0% -> 0%
where the time goes in v1:
time: 594 us; the launch traced here: 585 us
  waiting for transfers between devices  254 us (43%)
  matrix products  96 us (16%)
  local copies, waits for them, and re-layouts  93.6 us (16%)
  other arithmetic  74 us (12%)
  starting transfers between devices  51.4 us (9%)
  between operations  15.4 us (3%)
    psum x1, waiting for transfers between devices, body(): lax.psum(lax.psum((grad_msg, grad_in, grad_zr, grad_h, grad_query, grad_k...  112 us
    psum x1, waiting for transfers between devices, body(): lax.psum((grad_msg, grad_in, grad_zr, grad_h, grad_query, grad_key, grad_...  54.8 us
    all_to_all x1, waiting for transfers between devices, body(): lax.all_to_all(nb_grads.reshape(devices, cap_neigh, row_width), ('acct',...  51.2 us
    all_to_all x1, waiting for transfers between devices, body(): lax.all_to_all(nb_reply, ('acct', 'rep'), split_axis=0, concat_axis=0, ti...  30.5 us
    unnamed x105, local copies, waits for them, and re-layouts  27 us
    add x1, other arithmetic, body(): d_memory + jax.ops.segment_sum(got_nb_grads.reshape(-1, row_width), nb_ro...  23.1 us
    dot_general x1, matrix products, gru_forward(): jnp.dot(reset_state, u_h, preferred_element_type=jnp.float32)  19.8 us
    convert_element_type x1, other arithmetic, gru_backward(): d_update_in.astype(jnp.bfloat16)  17.9 us
  transfers between devices with their start and end apart: 10, of which 6 were waited for; matrix products, arithmetic and copies ran while one was open for 23% of the time, Pallas kernels for 0%

profile of v1, /device:TPU:0, one launch (start us, length us, event | category | flops | bytes accessed | tf_op | source)
XLA Modules:
  0.0 584.8 jit_solution(15583173649983513423)
XLA Ops:
  15.1 7.3 %all-to-all-start = ((s32[32,2,8]{2,1,0:T(2,128)}), s32[32,2,8]{2,1,0:T(2,128)S(1)}, u32[]{:S(2)}, u32[]{:S(2)}) async-start(s32[32,2,8]{2,1,0:T(2,128)} %copy.87), calls=%async_computation | async-start | bytes 65536 | tf_op jit(solution)/shard_map/all_to_all | solution.py:186
  29.2 9.1 %reduce-window.6 = s32[32,10,128]{2,1,0:T(8,128)S(1)} reduce-window(s32[32,10,128]{2,1,0:T(8,128)S(1)} %fusion.57, s32[]{:T(128)} %constant.17.clone.1), window={size=1x1x128 pad=0_0x0_0x127_0}, to_apply=%region_12.13 | reduce-window | flops 5201920 | bytes 327684 | tf_op jit(solution)/shard_map/reduce-window
  39.6 10.3 %fusion.117 = f32[8192,512]{0,1:T(8,128)} fusion(bf16[8192,256]{1,0:T(8,128)(2,1)} %param.17, bf16[256,512]{1,0:T(8,128)(2,1)S(1)} %copy-done), kind=kOutput, calls=%fused_computation.187 | convolution fusion | flops 2147483648 | bytes 21233664 | tf_op jit(solution)/shard_map/dot_general | solution.py:39
  50.0 6.5 %copy.91 = bf16[8192,256]{0,1:T(8,128)(2,1)} copy(bf16[8192,256]{1,0:T(8,128)(2,1)} %param.17) | data formatting | bytes 8388608 | tf_op args[0]
  57.3 5.3 scatter_custom_fusion.8
  63.3 5.8 all-to-all-start.2
  69.4 3.3 scatter_custom_fusion.2
  73.5 2.8 all-to-all-done.2
  76.4 3.3 all-to-all-start.1
  79.8 4.3 gather_fusion
  85.0 2.8 all-to-all-done.1
  87.9 3.1 all-to-all-start.4
  91.3 5.4 scatter_custom_fusion.7
  96.8 11.9 %fusion.113 = f32[8192,768]{0,1:T(8,128)} fusion(bf16[128,768]{1,0:T(8,128)(2,1)S(1)} %copy-done.27, f32[8192,128]{1,0:T(8,128)} %scatter_custom_fusion.7, f32[8192]{0:T(1024)S(1)} %broadcast_maximum_fusion), kind=kOutput, calls=%fused_computation.186 | convolution fusion | flops 1612709888 | bytes 29589504 | tf_op jit(solution)/shard_map/dot_general | solution.py:38
  108.7 19.8 %fusion.6 = (bf16[8192,256]{0,1:T(8,128)(2,1)}, f32[8192,256]{0,1:T(8,128)}) fusion(bf16[8192,256]{0,1:T(8,128)(2,1)S(1)} %copy-done.4, pred[8192]{0:T(1024)(128)(4,1)S(1)} %broadcast_compare_fusion, f32[8192,512]{0,1:T(8,128)} %fusion.117, f32[8192,768]{0,1:T(8,128)} %fusion.113, bf16[256,256]{1,0:T(8,128)(2,1)S(1)} %copy-done.44), kind=kOutput, calls=%fused_computation.32 | convolution fusion | flops 1113587712 | bytes 63053824 | tf_op jit(solution)/shard_map/dot_general | solution.py:48
  128.5 6.4 %copy.104 = bf16[8192,256]{1,0:T(8,128)(2,1)} copy(bf16[8192,256]{0,1:T(8,128)(2,1)} %get-tuple-element.78) | data formatting | bytes 8388608
  134.9 4.4 gather_fusion.1
  139.3 5.9 %all-to-all-start.3 = ((bf16[32,8,256]{2,1,0:T(8,128)(2,1)}), bf16[32,8,256]{2,1,0:T(8,128)(2,1)S(1)}, u32[]{:S(2)}, u32[]{:S(2)}) async-start(bf16[32,8,256]{2,1,0:T(8,128)(2,1)} %bitcast.11), calls=%async_computation.3 | async-start | bytes 262144 | tf_op jit(solution)/shard_map/all_to_all | solution.py:218
  145.9 9.5 %gather_fusion.3 = bf16[2560,256]{1,0:T(8,128)(2,1)} fusion(bf16[8192,256]{1,0:T(8,128)(2,1)} %copy.104, s32[3072]{0:T(1024)S(1)} %pad_clamp_fusion), kind=kCustom, calls=%fused_computation.3 | custom fusion | bytes 2631680 | tf_op jit(solution)/shard_map/gather | solution.py:216
  155.4 16.5 %all-to-all-start.5 = ((bf16[32,80,256]{2,1,0:T(8,128)(2,1)}), bf16[32,80,256]{2,1,0:T(8,128)(2,1)S(1)}, u32[]{:S(2)}, u32[]{:S(2)}) async-start(bf16[32,80,256]{2,1,0:T(8,128)(2,1)} %bitcast.15), calls=%async_computation.5 | async-start | bytes 2621440 | tf_op jit(solution)/shard_map/all_to_all | solution.py:219
  173.2 30.5 %all-to-all-done.5 = bf16[32,80,256]{2,1,0:T(8,128)(2,1)S(1)} async-done(((bf16[32,80,256]{2,1,0:T(8,128)(2,1)}), bf16[32,80,256]{2,1,0:T(8,128)(2,1)S(1)}, u32[]{:S(2)}, u32[]{:S(2)}) %all-to-all-start.5) | async-done | bytes 1310752 | tf_op jit(solution)/shard_map/all_to_all | solution.py:219
  203.7 4.1 gather_fusion.4
  213.4 1.7 scatter_custom_fusion.9
  215.1 3.6 all-to-all-start.6
  219.9 1.8 multiply_convert_fusion.1
  221.7 1.8 multiply_convert_fusion.2
  226.0 9.7 %scatter_custom_fusion.10 = f32[2560,256]{1,0:T(8,128)} fusion(s32[1280]{0:T(1024)} %copy-done.37, f32[1280,256]{1,0:T(8,128)S(1)} %convolution_add_fusion.1, f32[]{:T(128)} %constant.14.clone.1), kind=kCustom, calls=%fused_computation.66 | custom fusion | bytes 2621952 | tf_op jit(solution)/shard_map/scatter | solution.py:230
  235.7 5.8 all-to-all-start.7
  244.4 1.8 fusion.69
  246.2 2.2 fusion.44
  248.3 2.2 fusion.47
  250.5 51.2 %all-to-all-done.7 = f32[32,80,256]{2,1,0:T(8,128)S(1)} async-done(((f32[32,80,256]{2,1,0:T(8,128)}), f32[32,80,256]{2,1,0:T(8,128)S(1)}, u32[]{:S(2)}, u32[]{:S(2)}) %all-to-all-start.7) | async-done | bytes 2621472 | tf_op jit(solution)/shard_map/all_to_all | solution.py:240
  301.7 23.1 %scatter_custom_fusion.11 = f32[8192,256]{1,0:T(8,128)} fusion(s32[2816]{0:T(1024)} %add_reduce_fusion, f32[]{:T(128)} %constant.14.clone.1, f32[2560,256]{1,0:T(8,128)S(1)} %bitcast.149, f32[]{:T(128)} %constant.74, f32[256,256]{1,0:T(8,128)S(1)} %bitcast.155), kind=kCustom, calls=%fused_computation.53 | custom fusion | flops 1441792 | bytes 11273216 | tf_op jit(solution)/shard_map/add | solution.py:251
  324.8 9.0 %copy.103 = f32[8192,256]{0,1:T(8,128)} copy(f32[8192,256]{1,0:T(8,128)} %scatter_custom_fusion.11) | data formatting | bytes 16777216 | tf_op jit(solution)/shard_map/add | solution.py:251
  333.8 17.9 %fusion.10 = (bf16[8192,256]{0,1:T(8,128)(2,1)}, bf16[8192,256]{0,1:T(8,128)(2,1)}) fusion(f32[8192,256]{0,1:T(8,128)} %get-tuple-element.79, bf16[8192,256]{0,1:T(8,128)(2,1)} %copy.91, f32[8192,256]{0,1:T(8,128)} %copy.103, pred[8192]{0:T(1024)(128)(4,1)S(1)} %copy-done.36, f32[8192,512]{0,1:T(8,128)} %fusion.117, f32[8192,768]{0,1:T(8,128)} %fusion.113), kind=kLoop, calls=%fused_computation.36 | loop fusion | flops 35651584 | bytes 46145536 | tf_op jit(solution)/shard_map/convert_element_type | solution.py:66
  351.7 10.3 %fusion.110 = f32[256,256]{1,0:T(8,128)} fusion(bf16[8192,256]{0,1:T(8,128)(2,1)} %get-tuple-element.71, bf16[8192,256]{0,1:T(8,128)(2,1)S(1)} %copy-done.5, f32[8192,512]{0,1:T(8,128)} %fusion.117, f32[8192,768]{0,1:T(8,128)} %fusion.113), kind=kOutput, calls=%fused_computation.185 | convolution fusion | flops 1088421888 | bytes 25427968 | tf_op jit(solution)/shard_map/dot_general | solution.py:61
  362.0 9.3 %fusion.3 = bf16[8192,256]{0,1:T(8,128)(2,1)} fusion(bf16[8192,256]{0,1:T(8,128)(2,1)S(1)} %copy-done.5, bf16[256,256]{1,0:T(8,128)(2,1)S(1)} %copy-done.45, bf16[8192,256]{0,1:T(8,128)(2,1)S(1)} %copy-done.7, f32[8192,512]{0,1:T(8,128)} %fusion.117, f32[8192,768]{0,1:T(8,128)} %fusion.113), kind=kOutput, calls=%fused_computation.28 | convolution fusion | flops 1094713344 | bytes 29491200 | tf_op jit(solution)/shard_map/dot_general | solution.py:62
  371.4 9.0 %fusion.23 = f32[128,768]{1,0:T(8,128)} fusion(bf16[8192,256]{0,1:T(8,128)(2,1)S(1)} %copy-done.7, bf16[8192,256]{0,1:T(8,128)(2,1)} %fusion.3, bf16[8192,256]{0,1:T(8,128)(2,1)S(1)} %copy-done.6, f32[8192,128]{1,0:T(8,128)S(1)} %copy-done.3, f32[8192]{0:T(1024)S(1)} %copy-done.26), kind=kOutput, calls=%fused_computation.52 | convolution fusion | flops 1650458624 | bytes 17203200 | tf_op jit(solution)/shard_map/dot_general | solution.py:68
  380.5 6.7 %convolution_divide_fusion = f32[8192,128]{1,0:T(8,128)} fusion(bf16[128,768]{1,0:T(8,128)(2,1)S(1)} %copy-done.28, bf16[8192,256]{0,1:T(8,128)(2,1)S(1)} %copy-done.8, bf16[8192,256]{0,1:T(8,128)(2,1)S(1)} %copy-done.46, bf16[8192,256]{0,1:T(8,128)(2,1)S(1)} %copy-done.6, f32[8192]{0:T(1024)S(1)} %copy-done.26), kind=kOutput, calls=%fused_computation.29 | convolution fusion | flops 1649410048 | bytes 17006592 | tf_op jit(solution)/shard_map/dot_general | solution.py:70
  387.2 5.4 fusion.33
  392.6 3.3 gather_fusion.5
  397.2 54.8 %all-reduce.7.cloned.1.call-done = (f32[512,128]{1,0:T(8,128)}, f32[128,768]{1,0:T(8,128)}, f32[256,512]{0,1:T(8,128)}, f32[256,256]{1,0:T(8,128)}, f32[256,256]...) async-done(((f32[512,128]{1,0:T(8,128)}, f32[128,768]{1,0:T(8,128)}, f32[256,512]{0,1:T(8,128)}, f32[256,256]{1,0:T(8,128)}, f32[256,256]{1,0:T(8,128)}, ...) | async-done | bytes 2228240 | tf_op jit(solution)/shard_map/psum | solution.py:260
  453.2 112.2 %all-reduce.5.cloned.1.call-done = (f32[512,128]{1,0:T(8,128)}, f32[128,768]{1,0:T(8,128)}, f32[256,512]{0,1:T(8,128)}, f32[256,256]{1,0:T(8,128)}, f32[256,256]...) async-done(((f32[512,128]{1,0:T(8,128)}, f32[128,768]{1,0:T(8,128)}, f32[256,512]{0,1:T(8,128)}, f32[256,256]{1,0:T(8,128)}, f32[256,256]{1,0:T(8,128)}, ...) | async-done | bytes 2228240 | tf_op jit(solution)/shard_map/psum | solution.py:259
  565.4 2.0 copy.105
  567.4 1.7 copy.171
  569.1 1.8 copy.172
  570.9 1.7 copy.173
  572.5 1.7 copy.174
  (198 shorter events, 39.8 us)
Async XLA Ops:
  7.2 32.5 %copy-start = (bf16[256,512]{1,0:T(8,128)(2,1)S(1)}, bf16[256,512]{1,0:T(8,128)(2,1)}, u32[]{:S(2)}) copy-start(bf16[256,512]{1,0:T(8,128)(2,1)} %param.28) | copy-start | bytes 786436
  15.1 48.1 %all-to-all-start = ((s32[32,2,8]{2,1,0:T(2,128)}), s32[32,2,8]{2,1,0:T(2,128)S(1)}, u32[]{:S(2)}, u32[]{:S(2)}) async-start(s32[32,2,8]{2,1,0:T(2,128)} %copy.87), calls=%async_computation | async-start | bytes 65536 | tf_op jit(solution)/shard_map/all_to_all | solution.py:186
  39.6 132.4 %copy-start.37 = (s32[1280]{0:T(1024)}, s32[1280]{0:T(1024)S(1)}, u32[]{:S(2)}) copy-start(s32[1280]{0:T(1024)S(1)} %fusion.91) | copy-start | bytes 15364
  49.9 41.1 %copy-start.43 = (bf16[512,128]{1,0:T(8,128)(2,1)S(1)}, bf16[512,128]{1,0:T(8,128)(2,1)}, u32[]{:S(2)}) copy-start(bf16[512,128]{1,0:T(8,128)(2,1)} %param.26) | copy-start | bytes 393220
  49.9 46.8 %copy-start.27 = (bf16[128,768]{1,0:T(8,128)(2,1)S(1)}, bf16[128,768]{1,0:T(8,128)(2,1)}, u32[]{:S(2)}) copy-start(bf16[128,768]{1,0:T(8,128)(2,1)} %param.27) | copy-start | bytes 589828
  63.3 13.1 %all-to-all-start.2 = ((s32[32,2,8]{2,1,0:T(2,128)}), s32[32,2,8]{2,1,0:T(2,128)S(1)}, u32[]{:S(2)}, u32[]{:S(2)}) async-start(s32[32,2,8]{2,1,0:T(2,128)} %copy.90), calls=%async_computation.2 | async-start | bytes 65536 | tf_op jit(solution)/shard_map/all_to_all | solution.py:187
  69.2 39.4 %copy-start.40 = (f32[512]{0:T(512)}, f32[512]{0:T(512)S(1)}, u32[]{:S(2)}) copy-start(f32[512]{0:T(512)S(1)} %reshape.286) | copy-start | bytes 6148
  72.8 35.9 %copy-start.35 = (pred[8192]{0:T(1024)(128)(4,1)}, pred[8192]{0:T(1024)(128)(4,1)S(1)}, u32[]{:S(2)}) copy-start(pred[8192]{0:T(1024)(128)(4,1)S(1)} %broadcast_compare_fusion) | copy-start | bytes 24580
  72.8 35.8 %copy-start.25 = (f32[8192]{0:T(1024)}, f32[8192]{0:T(1024)S(1)}, u32[]{:S(2)}) copy-start(f32[8192]{0:T(1024)S(1)} %broadcast_maximum_fusion) | copy-start | bytes 98308
  73.4 14.4 %copy-start.38 = (s32[1024]{0:T(1024)}, s32[1024]{0:T(1024)S(1)}, u32[]{:S(2)}) copy-start(s32[1024]{0:T(1024)S(1)} %pad_clamp_fusion.4) | copy-start | bytes 12292
  76.4 11.5 %all-to-all-start.1 = ((bf16[32,2,8,128]{3,2,1,0:T(8,128)(2,1)}), bf16[32,2,8,128]{3,2,1,0:T(8,128)(2,1)S(1)}, u32[]{:S(2)}, u32[]{:S(2)}) async-start(bf16[32,2,8,128]{3,2,1,0:T(8,128)(2,1)} %pad_maximum_fusion.6), calls=%async_computation.1 | async-start | bytes 262144 | tf_op jit(solution)/shard_map/all_to_all | solution.py:198
  84.1 24.5 %copy-start.23 = (bf16[512,256]{1,0:T(8,128)(2,1)}, bf16[512,256]{1,0:T(8,128)(2,1)S(1)}, u32[]{:S(2)}) copy-start(bf16[512,256]{1,0:T(8,128)(2,1)S(1)} %gather_fusion) | copy-start | bytes 786436
  85.0 23.6 %copy-start.31 = (bf16[512,128]{1,0:T(8,128)(2,1)}, bf16[512,128]{1,0:T(8,128)(2,1)S(1)}, u32[]{:S(2)}) copy-start(bf16[512,128]{1,0:T(8,128)(2,1)S(1)} %cosine_convert_fusion) | copy-start | bytes 393220
  87.9 20.8 %copy-start.29 = (bf16[32,2,8,128]{3,2,1,0:T(8,128)(2,1)}, bf16[32,2,8,128]{3,2,1,0:T(8,128)(2,1)S(1)}, u32[]{:S(2)}) copy-start(bf16[32,2,8,128]{3,2,1,0:T(8,128)(2,1)S(1)} %all-to-all-done.1) | copy-start | bytes 393220
  87.9 51.4 %all-to-all-start.4 = ((s32[32,1,80]{2,1,0:T(1,128)}), s32[32,1,80]{2,1,0:T(1,128)S(1)}, u32[]{:S(2)}, u32[]{:S(2)}) async-start(s32[32,1,80]{2,1,0:T(1,128)} %all_to_all.31), calls=%async_computation.4 | async-start | bytes 32768 | tf_op jit(solution)/shard_map/all_to_all | solution.py:188
  91.3 17.3 %copy-start.21 = (f32[512,128]{1,0:T(8,128)}, f32[512,128]{1,0:T(8,128)S(1)}, u32[]{:S(2)}) copy-start(f32[512,128]{1,0:T(8,128)S(1)} %fusion.59) | copy-start | bytes 786436
  96.8 11.9 %copy-start.4 = (bf16[8192,256]{0,1:T(8,128)(2,1)S(1)}, bf16[8192,256]{0,1:T(8,128)(2,1)}, u32[]{:S(2)}) copy-start(bf16[8192,256]{0,1:T(8,128)(2,1)} %copy.91) | copy-start | bytes 12582916
  96.8 11.9 %copy-start.44 = (bf16[256,256]{1,0:T(8,128)(2,1)S(1)}, bf16[256,256]{1,0:T(8,128)(2,1)}, u32[]{:S(2)}) copy-start(bf16[256,256]{1,0:T(8,128)(2,1)} %param.29) | copy-start | bytes 393220
  134.9 37.0 %copy-start.16 = (bf16[128,256]{1,0:T(8,128)(2,1)S(1)}, bf16[128,256]{1,0:T(8,128)(2,1)}, u32[]{:S(2)}) copy-start(bf16[128,256]{1,0:T(8,128)(2,1)} %param.33) | copy-start | bytes 196612
  134.9 38.0 %copy-start.18 = (bf16[256,256]{1,0:T(8,128)(2,1)S(1)}, bf16[256,256]{1,0:T(8,128)(2,1)}, u32[]{:S(2)}) copy-start(bf16[256,256]{1,0:T(8,128)(2,1)} %param.30) | copy-start | bytes 393220
  139.3 16.2 %all-to-all-start.3 = ((bf16[32,8,256]{2,1,0:T(8,128)(2,1)}), bf16[32,8,256]{2,1,0:T(8,128)(2,1)S(1)}, u32[]{:S(2)}, u32[]{:S(2)}) async-start(bf16[32,8,256]{2,1,0:T(8,128)(2,1)} %bitcast.11), calls=%async_computation.3 | async-start | bytes 262144 | tf_op jit(solution)/shard_map/all_to_all | solution.py:218
  145.9 61.9 %copy-start.20 = (bf16[256,256]{1,0:T(8,128)(2,1)S(1)}, bf16[256,256]{1,0:T(8,128)(2,1)}, u32[]{:S(2)}) copy-start(bf16[256,256]{1,0:T(8,128)(2,1)} %param.32) | copy-start | bytes 393220
  155.4 53.6 %copy-start.19 = (bf16[256,256]{1,0:T(8,128)(2,1)S(1)}, bf16[256,256]{1,0:T(8,128)(2,1)}, u32[]{:S(2)}) copy-start(bf16[256,256]{1,0:T(8,128)(2,1)} %param.31) | copy-start | bytes 393220
  155.4 48.3 %all-to-all-start.5 = ((bf16[32,80,256]{2,1,0:T(8,128)(2,1)}), bf16[32,80,256]{2,1,0:T(8,128)(2,1)S(1)}, u32[]{:S(2)}, u32[]{:S(2)}) async-start(bf16[32,80,256]{2,1,0:T(8,128)(2,1)} %bitcast.15), calls=%async_computation.5 | async-start | bytes 2621440 | tf_op jit(solution)/shard_map/all_to_all | solution.py:219
  172.9 38.6 %copy-start.11 = (bf16[128,256]{1,0:T(8,128)(2,1)}, bf16[128,256]{1,0:T(8,128)(2,1)S(1)}, u32[]{:S(2)}) copy-start(bf16[128,256]{1,0:T(8,128)(2,1)S(1)} %gather_fusion.2) | copy-start | bytes 196612
  215.1 20.6 %all-to-all-start.6 = ((f32[32,8,256]{2,1,0:T(8,128)}), f32[32,8,256]{2,1,0:T(8,128)S(1)}, u32[]{:S(2)}, u32[]{:S(2)}) async-start(f32[32,8,256]{2,1,0:T(8,128)} %bitcast.25), calls=%async_computation.6 | async-start | bytes 524288 | tf_op jit(solution)/shard_map/all_to_all | solution.py:233
  219.9 21.7 %copy-start.33 = (s32[32,1,8]{2,1,0:T(1,128)S(1)}, s32[32,1,8]{2,1,0:T(1,128)}, u32[]{:S(2)}) copy-start(s32[32,1,8]{2,1,0:T(1,128)} %get-tuple-element.72) | copy-start | bytes 3076
  235.7 66.0 %all-to-all-start.7 = ((f32[32,80,256]{2,1,0:T(8,128)}), f32[32,80,256]{2,1,0:T(8,128)S(1)}, u32[]{:S(2)}, u32[]{:S(2)}) async-start(f32[32,80,256]{2,1,0:T(8,128)} %bitcast.29), calls=%async_computation.7 | async-start | bytes 5242880 | tf_op jit(solution)/shard_map/all_to_all | solution.py:240
  241.6 210.3 %all-reduce.7.cloned.1.call-start = ((), (), s32[]{:S(2)}) async-start(), calls=%async_computation.9 | async-start | bytes 4456448 | tf_op jit(solution)/shard_map/psum | solution.py:260
  324.8 9.0 %copy-start.36 = (pred[8192]{0:T(1024)(128)(4,1)S(1)}, pred[8192]{0:T(1024)(128)(4,1)}, u32[]{:S(2)}) copy-start(pred[8192]{0:T(1024)(128)(4,1)} %copy-done.35) | copy-start | bytes 24580
  333.8 17.9 %copy-start.5 = (bf16[8192,256]{0,1:T(8,128)(2,1)S(1)}, bf16[8192,256]{0,1:T(8,128)(2,1)}, u32[]{:S(2)}) copy-start(bf16[8192,256]{0,1:T(8,128)(2,1)} %copy.91) | copy-start | bytes 12582916
  351.7 10.3 %copy-start.7 = (bf16[8192,256]{0,1:T(8,128)(2,1)S(1)}, bf16[8192,256]{0,1:T(8,128)(2,1)}, u32[]{:S(2)}) copy-start(bf16[8192,256]{0,1:T(8,128)(2,1)} %get-tuple-element.71) | copy-start | bytes 12582916
  351.7 10.3 %copy-start.45 = (bf16[256,256]{1,0:T(8,128)(2,1)S(1)}, bf16[256,256]{1,0:T(8,128)(2,1)}, u32[]{:S(2)}) copy-start(bf16[256,256]{1,0:T(8,128)(2,1)} %param.29) | copy-start | bytes 393220
  362.0 9.3 %copy-start.3 = (f32[8192,128]{1,0:T(8,128)S(1)}, f32[8192,128]{1,0:T(8,128)}, u32[]{:S(2)}) copy-start(f32[8192,128]{1,0:T(8,128)} %scatter_custom_fusion.7) | copy-start | bytes 12582916
  362.0 9.4 %copy-start.6 = (bf16[8192,256]{0,1:T(8,128)(2,1)S(1)}, bf16[8192,256]{0,1:T(8,128)(2,1)}, u32[]{:S(2)}) copy-start(bf16[8192,256]{0,1:T(8,128)(2,1)} %get-tuple-element.70) | copy-start | bytes 12582916
  362.0 9.4 %copy-start.26 = (f32[8192]{0:T(1024)S(1)}, f32[8192]{0:T(1024)}, u32[]{:S(2)}) copy-start(f32[8192]{0:T(1024)} %copy-done.25) | copy-start | bytes 98308
  371.4 9.0 %copy-start.8 = (bf16[8192,256]{0,1:T(8,128)(2,1)S(1)}, bf16[8192,256]{0,1:T(8,128)(2,1)}, u32[]{:S(2)}) copy-start(bf16[8192,256]{0,1:T(8,128)(2,1)} %get-tuple-element.71) | copy-start | bytes 12582916
  371.4 9.0 %copy-start.28 = (bf16[128,768]{1,0:T(8,128)(2,1)S(1)}, bf16[128,768]{1,0:T(8,128)(2,1)}, u32[]{:S(2)}) copy-start(bf16[128,768]{1,0:T(8,128)(2,1)} %param.27) | copy-start | bytes 589828
  371.4 9.0 %copy-start.46 = (bf16[8192,256]{0,1:T(8,128)(2,1)S(1)}, bf16[8192,256]{0,1:T(8,128)(2,1)}, u32[]{:S(2)}) copy-start(bf16[8192,256]{0,1:T(8,128)(2,1)} %fusion.3) | copy-start | bytes 12582916
  387.1 8.8 %copy-start.24 = (bf16[512,256]{1,0:T(8,128)(2,1)S(1)}, bf16[512,256]{1,0:T(8,128)(2,1)}, u32[]{:S(2)}) copy-start(bf16[512,256]{1,0:T(8,128)(2,1)} %copy-done.23) | copy-start | bytes 786436
  387.2 8.8 %copy-start.30 = (bf16[32,2,8,128]{3,2,1,0:T(8,128)(2,1)S(1)}, bf16[32,2,8,128]{3,2,1,0:T(8,128)(2,1)}, u32[]{:S(2)}) copy-start(bf16[32,2,8,128]{3,2,1,0:T(8,128)(2,1)} %copy-done.29) | copy-start | bytes 393220
  387.2 8.8 %copy-start.32 = (bf16[512,128]{1,0:T(8,128)(2,1)S(1)}, bf16[512,128]{1,0:T(8,128)(2,1)}, u32[]{:S(2)}) copy-start(bf16[512,128]{1,0:T(8,128)(2,1)} %copy-done.31) | copy-start | bytes 393220
  387.2 8.8 %copy-start.41 = (f32[512]{0:T(512)S(1)}, f32[512]{0:T(512)}, u32[]{:S(2)}) copy-start(f32[512]{0:T(512)} %copy-done.40) | copy-start | bytes 6148
  387.2 190.4 %copy-start.1 = (bf16[256,512]{1,0:T(8,128)(2,1)S(1)}, bf16[256,512]{1,0:T(8,128)(2,1)}, u32[]{:S(2)}) copy-start(bf16[256,512]{1,0:T(8,128)(2,1)} %param.28) | copy-start | bytes 786436
  392.6 59.3 %copy-start.34 = (bf16[128,2,10]{0,1,2:T(2,128)(2,1)S(1)}, bf16[128,2,10]{0,1,2:T(2,128)(2,1)}, u32[]{:S(2)}) copy-start(bf16[128,2,10]{0,1,2:T(2,128)(2,1)} %get-tuple-element.77) | copy-start | bytes 15364
  392.6 59.5 %copy-start.14 = (bf16[128,10,2,128]{3,2,1,0:T(2,128)(2,1)S(1)}, bf16[128,10,2,128]{3,2,1,0:T(2,128)(2,1)}, u32[]{:S(2)}) copy-start(bf16[128,10,2,128]{3,2,1,0:T(2,128)(2,1)} %copy-done.13) | copy-start | bytes 1966084
  392.6 59.9 %copy-start.12 = (bf16[128,256]{1,0:T(8,128)(2,1)S(1)}, bf16[128,256]{1,0:T(8,128)(2,1)}, u32[]{:S(2)}) copy-start(bf16[128,256]{1,0:T(8,128)(2,1)} %copy-done.11) | copy-start | bytes 196612
  397.1 168.3 %all-reduce.5.cloned.1.call-start = ((), (), s32[]{:S(2)}) async-start(), calls=%async_computation.8 | async-start | bytes 4456448 | tf_op jit(solution)/shard_map/psum | solution.py:259
  (9 other events, 37.3 us)
Sparse Core Ops, SparseCore 0:
  397.2 54.6 all-reduce.6
  456.5 108.8 all-reduce.4
